TPU v7x, 32 devices: a whole 2x2x4 slice. The times are simulated.
32 devices in a mesh: region: 16 (over z, y, core), coord: 2 (over x).
Axes of the slice: x: 2, y: 2, z: 4, core: 2. Of those that a mesh axis runs over, the one named last changes fastest.
Arguments:
- right_side: float32 [2, 65536], P(None, ('region', 'coord')), may hold values from -6 to 6
- anchor: float32 [65536], P(('region', 'coord')), may hold values from 0.5 to 2
- blocks: float32 [512, 2, 128, 128], P(('region', 'coord')), may hold values from 2.734375e-05 to 0.02734375
- tile_nbr: int32 [512, 2], P(('region', 'coord')), may hold values from 0 to 31
- cut_cells: int32 [32, 32, 128], P(('region', 'coord')), may hold values from 0 to 2047
- cut_weight: float32 [32, 32, 128], P(('region', 'coord')), may hold values from 0 to 1, as said below
- pin_cell: int32 [131072], P(('region', 'coord')), may hold values from 0 to 2047
- pin_net: int32 [131072], P(('region', 'coord')), may hold values from 0 to 4095, as said below
- star_weight: float32 [4096], replicated, may hold values from 0.2 to 2
Outputs:
- positions: float32 [2, 65536], P(None, ('region', 'coord'))
- residual: float32 [2, 65536], P(None, ('region', 'coord'))
Inputs may be any that keep to these rules, and one draw needn't show every extreme that they name: cut_weight[d, p, s] equals cut_weight[p, d, s], and it is 0 where p equals d. Every net number appears exactly 32 times; net n is owned by partition n // 128, and pin_net[d * 4096 + o * 128 + s] is a net owned by partition o for every partition d, owner o and s below 128.
All inputs are finite; a program needn't handle non-finite values.
Results may differ from a plain program's by a relative error of at most 0.00021.
Values sent between devices are 32-bit elements; how exact they have to be, the bound alone decides.
A program may use at most 128 MiB of HBM per device.

v0:
```python
import functools

import jax
import jax.numpy as jnp
from jax import lax
from jax.experimental import pallas as pl
from jax.experimental.pallas import tpu as pltpu
from jax.sharding import PartitionSpec as P

FANOUT = 32
ITERS = 3
LANES = 128
GROUP = 4
MESH = pl.DeviceIdType.MESH
F32 = jnp.float32
BF16 = jnp.bfloat16

NN = (((1,), (0,)), ((), ()))
NT = (((1,), (1,)), ((), ()))


def mm(a, b, dims=NN):
    return lax.dot_general(a, b, dims, preferred_element_type=F32)


def pieces(x):
    high = x.astype(BF16)
    low = (x - high.astype(F32)).astype(BF16)
    return high, low


def kernel(
    regions,
    halves,
    rs_ref,
    anchor_ref,
    blocks_ref,
    nbr_row_ref,
    cut_cell_ref,
    cut_w_ref,
    pin_cell_ref,
    pin_net_ref,
    star_w_ref,
    out_ref,
    onehot,
    himask,
    block_buf,
    nethot,
    quad,
    lhs_b,
    lhs_f,
    back,
    front,
    send_star,
    recv_star,
    send_cut,
    recv_cut,
    send2,
    recv2,
    vec_send,
    vec_recv,
    spr_send,
    spr_recv,
    sems,
):
    count = regions * halves
    tiles = anchor_ref.shape[0]
    cut_groups = count // GROUP
    pin_chunks = pin_cell_ref.shape[0]
    pin_groups = pin_chunks // GROUP
    per_chunk = count // pin_chunks
    wide = GROUP * LANES
    my_region = lax.axis_index("region")
    my_half = lax.axis_index("coord")
    me = my_region * halves + my_half
    partner = (my_region, 1 - my_half)

    def each_other(act):
        act(my_region * halves + 1 - my_half, partner)

        @pl.loop(1, regions, unroll=True if regions <= 16 else 4)
        def _(step):
            region = my_region + step
            region = jnp.where(region >= regions, region - regions, region)
            for flip in range(halves):
                half = my_half if flip == 0 else 1 - my_half
                act(region * halves + half, (region, half))

    def over_groups(groups, body):
        if groups <= 8:
            for group in range(groups):
                body(group)
        else:
            pl.loop(0, groups, unroll=4)(body)

    def sum_groups(groups, body, total):
        if groups <= 8:
            for group in range(groups):
                total = body(group, total)
            return total
        return lax.fori_loop(0, groups, body, total, unroll=4)

    barrier = pltpu.get_barrier_semaphore()

    def greet(other, device):
        pl.semaphore_signal(barrier, inc=1, device_id=device, device_id_type=MESH)

    each_other(greet)
    block_copy = pltpu.make_async_copy(blocks_ref, block_buf, sems.at[10 * ITERS])
    block_copy.start()

    iota_lo = lax.broadcasted_iota(jnp.int32, (LANES, LANES), 0)
    iota_hi = lax.broadcasted_iota(jnp.int32, (tiles, LANES), 0)
    iota_net = lax.broadcasted_iota(jnp.int32, (per_chunk * LANES, LANES), 0)
    lane = lax.broadcasted_iota(jnp.int32, (1, LANES), 1)

    def put_onehot(group, place, cells):
        lanes = slice(place * LANES, (place + 1) * LANES)
        low = lax.bitwise_and(cells, LANES - 1)
        high = lax.shift_right_logical(cells, 7)
        onehot[group, :, lanes] = (iota_lo == low).astype(F32).astype(BF16)
        himask[group, :, lanes] = (iota_hi == high).astype(F32)

    def hot_pins(group):
        for place in range(GROUP):
            chunk = group * GROUP + place
            put_onehot(cut_groups + group, place, pin_cell_ref[pl.ds(chunk, 1), :])
            net = pin_net_ref[pl.ds(chunk, 1), :] - chunk * (per_chunk * LANES)
            nethot[chunk] = (iota_net == net).astype(F32).astype(BF16)

    def hot_cut(group):
        for place in range(GROUP):
            put_onehot(group, place, cut_cell_ref[pl.ds(group * GROUP + place, 1), :])

    over_groups(pin_groups, hot_pins)

    def hold_blocks():
        block_copy.wait()

        @pl.loop(0, tiles, unroll=4)
        def _(tile):
            for k in range(2):
                high, low = pieces(block_buf[2 * tile + k])
                lanes = slice(k * LANES, (k + 1) * LANES)
                quad[tile, :LANES, lanes] = high
                quad[tile, LANES:, lanes] = low

        ones_row = jnp.where(lax.broadcasted_iota(jnp.int32, (8, 2 * LANES), 0) == 4, 1.0, 0.0)
        for tile in range(tiles):
            lhs_b[tile] = ones_row
            lhs_f[tile] = ones_row

    shift = my_half * tiles
    span = 2 * tiles
    rel_row = nbr_row_ref[...] - shift
    rel_row = jnp.where(rel_row < 0, rel_row + span, rel_row)
    on_diagonal = lax.broadcasted_iota(jnp.int32, (tiles, tiles), 0) == lax.broadcasted_iota(
        jnp.int32, (tiles, tiles), 1
    )
    rel_col = [
        jnp.sum(
            jnp.where(on_diagonal, rel_row[k : k + 1, :].astype(F32), 0.0), axis=1, keepdims=True
        ).astype(jnp.int32)
        for k in range(2)
    ]
    spread_hot = [
        (lax.broadcasted_iota(jnp.int32, (span, tiles), 0) == rel_row[k : k + 1, :])
        .astype(F32)
        .astype(BF16)
        for k in range(2)
    ]
    select_hot = [
        (lax.broadcasted_iota(jnp.int32, (tiles, span), 1) == rel_col[k])
        .astype(F32)
        .astype(BF16)
        for k in range(2)
    ]
    my_weight = star_w_ref[pl.ds(me, 1), :] * (1.0 / FANOUT)

    def rows8(first, second):
        fh, fl = pieces(first)
        sh, sl = pieces(second)
        stacked = jnp.concatenate(
            [x.astype(F32) for x in (fh, sh, fl, sl)]
            + [jnp.zeros((4, first.shape[1]), F32)],
            axis=0,
        )
        return stacked.astype(BF16)

    def gathered(group, left):
        got = mm(left, onehot[group])
        got = got[: 2 * tiles] + got[2 * tiles :]
        mask = himask[group]
        return [
            jnp.sum(got[c * tiles : (c + 1) * tiles] * mask, axis=0, keepdims=True)
            for c in range(2)
        ]

    def scattered(group, rows):
        mask = himask[group]
        spread = jnp.concatenate([mask * row for row in rows], axis=0)
        high, low = pieces(spread)
        both = mm(jnp.concatenate([high, low], axis=0), onehot[group], NT)
        rows_all = len(rows) * tiles
        return both[:rows_all] + both[rows_all:]

    def dot_rows(values):
        row = jnp.zeros((1, LANES), F32)
        for k, (a, b) in enumerate(values):
            total = jnp.sum(jnp.sum(a * b, axis=0, keepdims=True), axis=1, keepdims=True)
            row = jnp.where(lane == k, total, row)
        return row

    def halves_of(x):
        return x[:tiles], x[tiles:]

    def send_all(source_of, target, slot):
        def send(other, device):
            pltpu.make_async_remote_copy(
                src_ref=source_of(other),
                dst_ref=target.at[me],
                send_sem=sems.at[slot],
                recv_sem=sems.at[slot + 1],
                device_id=device,
                device_id_type=MESH,
            ).start()

        each_other(send)

    def wait_all(like, slot):
        part = like.at[pl.ds(0, count - 1)]
        pltpu.make_async_copy(part, part, sems.at[slot]).wait()

    def to_partner(source, target, slot):
        copy = pltpu.make_async_remote_copy(
            src_ref=source,
            dst_ref=target,
            send_sem=sems.at[slot],
            recv_sem=sems.at[slot + 1],
            device_id=partner,
            device_id_type=MESH,
        )
        copy.start()
        return copy

    def operate(turn, vector, dots, degree=None):
        first = turn == 0
        last = turn == ITERS - 1
        terms = 3 if first else 2
        base = turn * 10
        if first:
            pl.semaphore_wait(barrier, count - 1)
        vec_send[turn] = vector
        vec_copy = to_partner(vec_send.at[turn], vec_recv.at[turn], base)
        high, low = pieces(vector)
        left = jnp.concatenate([high, low], axis=0)

        def star_values(group):
            rows = gathered(cut_groups + group, left)
            for place in range(GROUP):
                chunk = group * GROUP + place
                lanes = slice(place * LANES, (place + 1) * LANES)
                sums = mm(rows8(rows[0][:, lanes], rows[1][:, lanes]), nethot[chunk], NT)
                sums = sums[0:2] + sums[2:4]
                for r in range(per_chunk):
                    send_star[turn, chunk * per_chunk + r] = sums[:, r * LANES : (r + 1) * LANES]

        over_groups(pin_groups, star_values)
        send_all(lambda other: send_star.at[turn, other], recv_star.at[turn], base + 2)
        recv_star[turn, me] = send_star[turn, me]
        if first:
            over_groups(cut_groups, hot_cut)

        def cut_values(group):
            rows = gathered(group, left)
            for place in range(GROUP):
                lanes = slice(place * LANES, (place + 1) * LANES)
                send_cut[turn, group * GROUP + place] = jnp.concatenate(
                    [rows[0][:, lanes], rows[1][:, lanes]], axis=0
                )

        over_groups(cut_groups, cut_values)
        send_all(lambda other: send_cut.at[turn, other], recv_cut.at[turn], base + 8)
        recv_cut[turn, me] = send_cut[turn, me]

        if first:
            hold_blocks()
        parts = (*halves_of(high.astype(F32)), *halves_of(low.astype(F32)))
        for r, part in enumerate(parts):
            lhs_b[:, r, :LANES] = part
            lhs_b[:, r, LANES:] = part
        for tile in range(tiles):
            out = mm(lhs_b[tile].astype(BF16), quad[tile])
            pair = out[0:2] + out[2:4]
            for k in range(2):
                lanes = slice(k * LANES, (k + 1) * LANES)
                for c in range(2):
                    back[k, tile : tile + 1, c * LANES : (c + 1) * LANES] = pair[
                        c : c + 1, lanes
                    ]
                if first:
                    back[k, tile : tile + 1, 2 * LANES :] = out[4:5, lanes]
        cols = terms * LANES
        spread = jnp.zeros((span, cols), F32)
        for k in range(2):
            bh, bl = pieces(back[k, :, :cols])
            spread = spread + mm(spread_hot[k], bh) + mm(spread_hot[k], bl)
        local = [spread[:tiles, c * LANES : (c + 1) * LANES] for c in range(terms)]
        for c in range(terms):
            spr_send[turn, c * tiles : (c + 1) * tiles] = spread[
                tiles:, c * LANES : (c + 1) * LANES
            ]
        if not first:
            spr_send[turn, 2 * tiles :] = jnp.zeros((tiles, LANES), F32)
        spr_copy = to_partner(spr_send.at[turn], spr_recv.at[turn], base + 4)

        vec_copy.wait()
        other = vec_recv[turn]
        whole = [
            jnp.concatenate([vector[c * tiles : (c + 1) * tiles], other[c * tiles : (c + 1) * tiles]], axis=0)
            for c in range(2)
        ]
        wh = [pieces(x) for x in whole]
        table = jnp.concatenate([wh[0][0], wh[1][0], wh[0][1], wh[1][1]], axis=1)
        for k in range(2):
            chosen = mm(select_hot[k], table)
            for r in range(4):
                lhs_f[:, r, k * LANES : (k + 1) * LANES] = chosen[:, r * LANES : (r + 1) * LANES]
        for tile in range(tiles):
            out = mm(lhs_f[tile].astype(BF16), quad[tile], NT)
            out = out[:, :LANES] + out[:, LANES:]
            pair = out[0:2] + out[2:4]
            for c in range(2):
                front[c, tile : tile + 1, :] = pair[c : c + 1]
            if first:
                front[2, tile : tile + 1, :] = out[4:5]
        local = [local[c] + front[c] for c in range(terms)]

        dots = dots()
        wait_all(recv_star.at[turn], base + 3)
        totals = jnp.sum(recv_star[turn], axis=0)
        if last:
            wait_all(recv_cut.at[turn], base + 9)
            across = jnp.sum(
                send_cut[turn] * recv_cut[turn] * cut_w_ref[...][:, None, :], axis=0
            )
            across = across + my_weight * totals * totals
            energy = []
            for c in range(2):
                own = vector[c * tiles : (c + 1) * tiles]
                inner = own * (degree[:tiles] * own - 2.0 * front[c])
                rows = jnp.sum(inner, axis=0, keepdims=True) - across[c : c + 1]
                energy.append(jnp.sum(rows, axis=1, keepdims=True))
            for c in range(2):
                dots = jnp.where(lane == 18 + c, energy[c], dots)
        send2[turn] = jnp.concatenate(
            [totals * my_weight, dots, jnp.zeros((1, LANES), F32)], axis=0
        )
        send_all(lambda other: send2.at[turn], recv2.at[turn], base + 6)
        recv2[turn, me] = send2[turn]

        if not last:
            wait_all(recv_cut.at[turn], base + 9)

        def cut_group(group, carry):
            weights = [cut_w_ref[pl.ds(group * GROUP + p, 1), :] for p in range(GROUP)]
            weight = jnp.concatenate(weights, axis=1)
            rows = [
                jnp.concatenate(
                    [recv_cut[turn, group * GROUP + p, c : c + 1, :] for p in range(GROUP)], axis=1
                )
                * weight
                for c in range(2)
            ]
            if first:
                rows.append(weight)
            return carry + scattered(group, rows)

        total = sum_groups(cut_groups, cut_group, jnp.zeros((terms * tiles, LANES), F32))

        def pin_weights(group, carry):
            row = []
            for place in range(GROUP):
                chunk = group * GROUP + place
                owners = [chunk * per_chunk + r for r in range(per_chunk)]
                own = jnp.concatenate([star_w_ref[pl.ds(o, 1), :] for o in owners], axis=1)
                got = mm(rows8(own, own), nethot[chunk])
                row.append(got[0:1] + got[2:3])
            return carry + scattered(cut_groups + group, [jnp.concatenate(row, axis=1)])

        if first:
            weighed = sum_groups(pin_groups, pin_weights, total[2 * tiles :])
        spr_copy.wait()
        wait_all(recv2.at[turn], base + 7)

        def pin_group(group, carry):
            rows = [[], []]
            for place in range(GROUP):
                chunk = group * GROUP + place
                owners = [chunk * per_chunk + r for r in range(per_chunk)]
                table = [
                    jnp.concatenate([recv2[turn, o, c : c + 1, :] for o in owners], axis=1)
                    for c in range(2)
                ]
                got = mm(rows8(*table), nethot[chunk])
                got = got[0:2] + got[2:4]
                for c in range(2):
                    rows[c].append(got[c : c + 1])
            return carry + scattered(
                cut_groups + group, [jnp.concatenate(r, axis=1) for r in rows]
            )

        total = sum_groups(pin_groups, pin_group, total[: 2 * tiles])
        if first:
            total = jnp.concatenate([total, weighed], axis=0)
        arrived = spr_recv[turn]
        both = jnp.concatenate(local, axis=0) + arrived[: terms * tiles] + total
        summed = jnp.sum(recv2[turn], axis=0)[2:3]
        wait_all(send_star.at[turn], base + 2)
        wait_all(send_cut.at[turn], base + 8)
        wait_all(recv2.at[turn], base + 6)
        return both, summed

    def pick(row, k):
        return jnp.sum(jnp.where(lane == k, row, 0.0), axis=1, keepdims=True)

    def stretch(pair):
        return jnp.concatenate(
            [jnp.broadcast_to(x, (tiles, LANES)) for x in pair], axis=0
        )

    def dots_of(pairs):
        return dot_rows([both for a, b in pairs for both in zip(halves_of(a), halves_of(b))])

    r = jnp.concatenate(
        [
            rs_ref[c : c + 1, t * LANES : (t + 1) * LANES]
            for c in range(2)
            for t in range(tiles)
        ],
        axis=0,
    )
    both, _ = operate(0, r, lambda: jnp.zeros((1, LANES), F32))
    degree = anchor_ref[...] + both[2 * tiles :]
    degree = jnp.concatenate([degree, degree], axis=0)
    w = degree * r - both[: 2 * tiles]
    x = jnp.zeros_like(r)
    p = s = z = None
    old_gamma = old_alpha = old_beta = beta = None
    for iteration in range(ITERS):
        if iteration + 1 < ITERS:
            pairs = [(r, r), (w, r)]
            if iteration + 2 == ITERS:
                pairs += [(r, s), (w, w), (w, s), (s, s), (w, z), (z, r), (z, s)]
            both, summed = operate(iteration + 1, w, functools.partial(dots_of, pairs), degree)
            q = degree * w - both
            gamma = [pick(summed, c) for c in range(2)]
            delta = [pick(summed, 2 + c) for c in range(2)]
        else:
            gamma, delta = [], []
            for c in range(2):
                rr, wr, rs, ww, ws, ss, wz, zr, zs, wq = [
                    pick(summed, 2 * k + c) for k in range(10)
                ]
                a, b = old_alpha[c], old_beta[c]
                ws_part = ww + b * ws
                gamma.append(
                    rr - 2.0 * a * (wr + b * rs) + a * a * (ws_part + b * (ws + b * ss))
                )
                w_next = wr - a * ws_part
                q_next = ww - a * (wq + b * wz)
                z_next = zr - a * (wz + b * zs)
                delta.append(w_next - a * (q_next + b * z_next))
        if iteration == 0:
            alpha = [gamma[c] / delta[c] for c in range(2)]
            p, s = r, w
            if iteration + 1 < ITERS:
                z = q
        else:
            beta = [gamma[c] / old_gamma[c] for c in range(2)]
            alpha = [
                gamma[c] / (delta[c] - beta[c] * gamma[c] / old_alpha[c]) for c in range(2)
            ]
            spread_beta = stretch(beta)
            p = r + spread_beta * p
            s = w + spread_beta * s
            if iteration + 1 < ITERS:
                z = q + spread_beta * z
        step = stretch(alpha)
        x = x + step * p
        r = r - step * s
        if iteration + 1 < ITERS:
            w = w - step * z
        old_gamma, old_alpha, old_beta = gamma, alpha, beta
    for c in range(2):
        for t in range(tiles):
            row = c * tiles + t
            lanes = slice(t * LANES, (t + 1) * LANES)
            out_ref[c : c + 1, lanes] = x[row : row + 1]
            out_ref[2 + c : 3 + c, lanes] = r[row : row + 1]


def per_device(
    regions,
    halves,
    right_side,
    anchor,
    blocks,
    tile_nbr,
    cut_cells,
    cut_weight,
    pin_cell,
    pin_net,
    star_weight,
):
    count = regions * halves
    tiles = blocks.shape[0]
    near = blocks.shape[1]
    pin_chunks = pin_cell.shape[0] // LANES
    per_chunk = count // pin_chunks
    groups = count // GROUP + pin_chunks // GROUP
    wide = GROUP * LANES
    vmem = pl.BlockSpec(memory_space=pltpu.VMEM)
    shape = jax.ShapeDtypeStruct((4, tiles * LANES), F32)
    joint = pl.pallas_call(
        functools.partial(kernel, regions, halves),
        out_shape=shape,
        in_specs=[vmem] * 2 + [pl.BlockSpec(memory_space=pl.ANY)] + [vmem] * 6,
        out_specs=vmem,
        scratch_shapes=[
            pltpu.VMEM((groups, LANES, wide), BF16),
            pltpu.VMEM((groups, tiles, wide), F32),
            pltpu.VMEM((tiles * near, LANES, LANES), F32),
            pltpu.VMEM((pin_chunks, per_chunk * LANES, LANES), BF16),
            pltpu.VMEM((tiles, 2 * LANES, 2 * LANES), BF16),
            pltpu.VMEM((tiles, 8, 2 * LANES), F32),
            pltpu.VMEM((tiles, 8, 2 * LANES), F32),
            pltpu.VMEM((2, tiles, 3 * LANES), F32),
            pltpu.VMEM((3, tiles, LANES), F32),
            pltpu.VMEM((ITERS, count, 2, LANES), F32),
            pltpu.VMEM((ITERS, count, 2, LANES), F32),
            pltpu.VMEM((ITERS, count, 2, LANES), F32),
            pltpu.VMEM((ITERS, count, 2, LANES), F32),
            pltpu.VMEM((ITERS, 4, LANES), F32),
            pltpu.VMEM((ITERS, count, 4, LANES), F32),
            pltpu.VMEM((ITERS, 2 * tiles, LANES), F32),
            pltpu.VMEM((ITERS, 2 * tiles, LANES), F32),
            pltpu.VMEM((ITERS, 3 * tiles, LANES), F32),
            pltpu.VMEM((ITERS, 3 * tiles, LANES), F32),
            pltpu.SemaphoreType.DMA((10 * ITERS + 1,)),
        ],
        compiler_params=pltpu.CompilerParams(
            collective_id=0, has_side_effects=True, vmem_limit_bytes=56 * 1024 * 1024
        ),
    )(
        right_side,
        anchor.reshape(tiles, LANES),
        blocks.reshape(tiles * near, LANES, LANES),
        tile_nbr.T,
        cut_cells[0],
        cut_weight[0],
        pin_cell.reshape(pin_chunks, LANES),
        pin_net.reshape(pin_chunks, LANES),
        star_weight.reshape(count, LANES),
    )
    return joint[:2], joint[2:]


def solution(mesh):
    return jax.shard_map(
        functools.partial(per_device, mesh.shape["region"], mesh.shape["coord"]),
        mesh=mesh,
        in_specs=(
            P(None, ("region", "coord")),
            P(("region", "coord")),
            P(("region", "coord"), None, None, None),
            P(("region", "coord"), None),
            P(("region", "coord"), None, None),
            P(("region", "coord"), None, None),
            P(("region", "coord")),
            P(("region", "coord")),
            P(),
        ),
        out_specs=(P(None, ("region", "coord")), P(None, ("region", "coord"))),
        check_vma=False,
    )
```

profile of v0, /device:TPU:0, one launch (start us, length us, event | category | flops | bytes accessed | tf_op | source)
XLA Modules:
  0.0 46.8 jit_solution(9466105749015777376)
XLA Ops:
  0.6 44.7 %shard_map.104 = f32[4,2048]{1,0:T(4,128)} custom-call(f32[2,2048]{1,0:T(2,128)} %rs_ref.1, f32[16,128]{1,0:T(8,128)} %bitcast.14, f32[32,128,128]{2,1,0:T(8,128)} %bitcast.8, s32[2,16]{1,0:T(2,128)} %bitcast.15, s32[32,128]{1,0:T(8,128)} %bitcast.9, f32[32,128]{1,0:T(8,128)} %bitcast.10, s32[32,128]{1,0:T(8,128)} %bitcast.11, s32[32,128]{1,0:T(8,128)} %bitcast.12, ...), custom_call_target="tpu_custom_call" | custom-call | tf_op jit(solution)/shard_map/pallas_call | solution.py:525
  45.3 1.5 %fusion = (f32[2,2048]{1,0:T(2,128)}, f32[2,2048]{1,0:T(2,128)}) fusion(f32[4,2048]{1,0:T(4,128)} %shard_map.104), kind=kLoop, calls=%fused_computation | loop fusion | bytes 65536 | tf_op jit(solution)/shard_map/slice | solution.py:566
where the time goes:
time: 47 us; the launch traced here: 46.8 us
  Pallas kernels  44.7 us (95%)
  local copies, waits for them, and re-layouts  1.46 us (3%)
  between operations  0.64 us (1%)
    pallas_call x1, Pallas kernels, per_device(): pl.pallas_call(functools.partial(kernel, regions, halves), out_shape=shap...  44.7 us
    slice x1, local copies, waits for them, and re-layouts, per_device(): return (joint[:2], joint[2:])  1.46 us

commit v1 on v0

--- a/solution.py
+++ b/solution.py
@@ -32,16 +32,24 @@
 def kernel(
     regions,
     halves,
+    rs_hbm,
+    anchor_hbm,
+    blocks_ref,
+    nbr_row_hbm,
+    cut_cell_hbm,
+    cut_w_hbm,
+    pin_cell_hbm,
+    pin_net_hbm,
+    star_w_hbm,
+    out_ref,
     rs_ref,
     anchor_ref,
-    blocks_ref,
     nbr_row_ref,
     cut_cell_ref,
     cut_w_ref,
     pin_cell_ref,
     pin_net_ref,
     star_w_ref,
-    out_ref,
     onehot,
     himask,
     block_buf,
@@ -57,13 +65,21 @@
     recv_cut,
     send2,
     recv2,
+    dot_send,
+    dot_recv,
+    star_energy,
     vec_send,
     vec_recv,
     spr_send,
     spr_recv,
     sems,
+    in_sems,
 ):
     count = regions * halves
+    first_owner = regions // 4
+    owner_regions = regions - 2 * first_owner
+    owners = owner_regions * halves
+    share = count // owners
     tiles = anchor_ref.shape[0]
     cut_groups = count // GROUP
     pin_chunks = pin_cell_ref.shape[0]
@@ -74,6 +90,8 @@
     my_half = lax.axis_index("coord")
     me = my_region * halves + my_half
     partner = (my_region, 1 - my_half)
+    owning = jnp.logical_and(my_region >= first_owner, my_region < first_owner + owner_regions)
+    my_share = (my_region - first_owner) * halves + my_half
 
     def each_other(act):
         act(my_region * halves + 1 - my_half, partner)
@@ -86,6 +104,26 @@
                 half = my_half if flip == 0 else 1 - my_half
                 act(region * halves + half, (region, half))
 
+    def each_owner(act):
+        mine = lax.rem(my_region + owner_regions - first_owner % owner_regions, owner_regions)
+
+        def at(step):
+            place = mine + step
+            return jnp.where(place >= owner_regions, place - owner_regions, place)
+
+        @pl.loop(1, owner_regions, unroll=True if regions <= 16 else 4)
+        def _(step):
+            place = at(step)
+            for flip in range(halves):
+                half = my_half if flip == 0 else 1 - my_half
+                act(place * halves + half, (place + first_owner, half))
+
+        act(mine * halves + 1 - my_half, (mine + first_owner, 1 - my_half))
+
+        @pl.when(jnp.logical_not(owning))
+        def _():
+            act(mine * halves + my_half, (mine + first_owner, my_half))
+
     def over_groups(groups, body):
         if groups <= 8:
             for group in range(groups):
@@ -106,8 +144,23 @@
         pl.semaphore_signal(barrier, inc=1, device_id=device, device_id_type=MESH)
 
     each_other(greet)
-    block_copy = pltpu.make_async_copy(blocks_ref, block_buf, sems.at[10 * ITERS])
-    block_copy.start()
+    load = {}
+    for k, (name, source, target) in enumerate(
+        (
+            ("pin_cell", pin_cell_hbm, pin_cell_ref),
+            ("pin_net", pin_net_hbm, pin_net_ref),
+            ("rs", rs_hbm, rs_ref),
+            ("cut_cell", cut_cell_hbm, cut_cell_ref),
+            ("nbr", nbr_row_hbm, nbr_row_ref),
+            ("star_w", star_w_hbm, star_w_ref),
+            ("cut_w", cut_w_hbm, cut_w_ref),
+            ("anchor", anchor_hbm, anchor_ref),
+            ("blocks", blocks_ref, block_buf),
+        )
+    ):
+        load[name] = pltpu.make_async_copy(source, target, in_sems.at[k])
+        load[name].start()
+    star_energy[...] = jnp.zeros_like(star_energy)
 
     iota_lo = lax.broadcasted_iota(jnp.int32, (LANES, LANES), 0)
     iota_hi = lax.broadcasted_iota(jnp.int32, (tiles, LANES), 0)
@@ -132,10 +185,12 @@
         for place in range(GROUP):
             put_onehot(group, place, cut_cell_ref[pl.ds(group * GROUP + place, 1), :])
 
+    load["pin_cell"].wait()
+    load["pin_net"].wait()
     over_groups(pin_groups, hot_pins)
 
     def hold_blocks():
-        block_copy.wait()
+        load["blocks"].wait()
 
         @pl.loop(0, tiles, unroll=4)
         def _(tile):
@@ -150,6 +205,7 @@
             lhs_b[tile] = ones_row
             lhs_f[tile] = ones_row
 
+    load["nbr"].wait()
     shift = my_half * tiles
     span = 2 * tiles
     rel_row = nbr_row_ref[...] - shift
@@ -175,7 +231,6 @@
         .astype(BF16)
         for k in range(2)
     ]
-    my_weight = star_w_ref[pl.ds(me, 1), :] * (1.0 / FANOUT)
 
     def rows8(first, second):
         fh, fl = pieces(first)
@@ -227,9 +282,13 @@
 
         each_other(send)
 
-    def wait_all(like, slot):
-        part = like.at[pl.ds(0, count - 1)]
+    def wait_all(like, slot, messages=count - 1):
+        part = like.at[pl.ds(0, messages)]
         pltpu.make_async_copy(part, part, sems.at[slot]).wait()
+
+    def for_owner(act):
+        pl.when(owning)(lambda: act(owners - 1))
+        pl.when(jnp.logical_not(owning))(lambda: act(owners))
 
     def to_partner(source, target, slot):
         copy = pltpu.make_async_remote_copy(
@@ -247,7 +306,7 @@
         first = turn == 0
         last = turn == ITERS - 1
         terms = 3 if first else 2
-        base = turn * 10
+        base = turn * 12
         if first:
             pl.semaphore_wait(barrier, count - 1)
         vec_send[turn] = vector
@@ -266,9 +325,25 @@
                     send_star[turn, chunk * per_chunk + r] = sums[:, r * LANES : (r + 1) * LANES]
 
         over_groups(pin_groups, star_values)
-        send_all(lambda other: send_star.at[turn, other], recv_star.at[turn], base + 2)
-        recv_star[turn, me] = send_star[turn, me]
+
+        def to_owner(owner, device):
+            pltpu.make_async_remote_copy(
+                src_ref=send_star.at[turn, pl.ds(owner * share, share)],
+                dst_ref=recv_star.at[turn, me],
+                send_sem=sems.at[base + 2],
+                recv_sem=sems.at[base + 3],
+                device_id=device,
+                device_id_type=MESH,
+            ).start()
+
+        each_owner(to_owner)
+
+        @pl.when(owning)
+        def _():
+            recv_star[turn, me] = send_star[turn, pl.ds(my_share * share, share)]
+
         if first:
+            load["cut_cell"].wait()
             over_groups(cut_groups, hot_cut)
 
         def cut_values(group):
@@ -336,15 +411,43 @@
                 front[2, tile : tile + 1, :] = out[4:5]
         local = [local[c] + front[c] for c in range(terms)]
 
-        dots = dots()
-        wait_all(recv_star.at[turn], base + 3)
-        totals = jnp.sum(recv_star[turn], axis=0)
+        if first:
+            load["star_w"].wait()
+
+        @pl.when(owning)
+        def _():
+            wait_all(recv_star.at[turn], base + 3)
+            totals = jnp.sum(recv_star[turn], axis=0)
+            weight = star_w_ref[pl.ds(my_share * share, share), :] * (1.0 / FANOUT)
+            weighted = totals * weight[:, None, :]
+            send2[turn] = weighted
+
+            def send(other, device):
+                pltpu.make_async_remote_copy(
+                    src_ref=send2.at[turn],
+                    dst_ref=recv2.at[turn, pl.ds(my_share * share, share)],
+                    send_sem=sems.at[base + 6],
+                    recv_sem=sems.at[base + 7],
+                    device_id=device,
+                    device_id_type=MESH,
+                ).start()
+
+            each_other(send)
+            recv2[turn, pl.ds(my_share * share, share)] = weighted
+            if last:
+                star_energy[...] = jnp.sum(weighted * totals, axis=0)
+
+        if first:
+            load["cut_w"].wait()
+            load["anchor"].wait()
+        else:
+            dots = dots()
+        wait_all(recv_cut.at[turn], base + 9)
         if last:
-            wait_all(recv_cut.at[turn], base + 9)
             across = jnp.sum(
                 send_cut[turn] * recv_cut[turn] * cut_w_ref[...][:, None, :], axis=0
             )
-            across = across + my_weight * totals * totals
+            across = across + star_energy[...]
             energy = []
             for c in range(2):
                 own = vector[c * tiles : (c + 1) * tiles]
@@ -353,14 +456,10 @@
                 energy.append(jnp.sum(rows, axis=1, keepdims=True))
             for c in range(2):
                 dots = jnp.where(lane == 18 + c, energy[c], dots)
-        send2[turn] = jnp.concatenate(
-            [totals * my_weight, dots, jnp.zeros((1, LANES), F32)], axis=0
-        )
-        send_all(lambda other: send2.at[turn], recv2.at[turn], base + 6)
-        recv2[turn, me] = send2[turn]
-
-        if not last:
-            wait_all(recv_cut.at[turn], base + 9)
+        if not first:
+            dot_send[turn] = dots
+            send_all(lambda other: dot_send.at[turn], dot_recv.at[turn], base + 10)
+            dot_recv[turn, me] = dots
 
         def cut_group(group, carry):
             weights = [cut_w_ref[pl.ds(group * GROUP + p, 1), :] for p in range(GROUP)]
@@ -382,8 +481,8 @@
             row = []
             for place in range(GROUP):
                 chunk = group * GROUP + place
-                owners = [chunk * per_chunk + r for r in range(per_chunk)]
-                own = jnp.concatenate([star_w_ref[pl.ds(o, 1), :] for o in owners], axis=1)
+                parts = [chunk * per_chunk + r for r in range(per_chunk)]
+                own = jnp.concatenate([star_w_ref[pl.ds(o, 1), :] for o in parts], axis=1)
                 got = mm(rows8(own, own), nethot[chunk])
                 row.append(got[0:1] + got[2:3])
             return carry + scattered(cut_groups + group, [jnp.concatenate(row, axis=1)])
@@ -391,15 +490,15 @@
         if first:
             weighed = sum_groups(pin_groups, pin_weights, total[2 * tiles :])
         spr_copy.wait()
-        wait_all(recv2.at[turn], base + 7)
+        for_owner(lambda n: wait_all(recv2.at[turn], base + 7, n * share))
 
         def pin_group(group, carry):
             rows = [[], []]
             for place in range(GROUP):
                 chunk = group * GROUP + place
-                owners = [chunk * per_chunk + r for r in range(per_chunk)]
+                parts = [chunk * per_chunk + r for r in range(per_chunk)]
                 table = [
-                    jnp.concatenate([recv2[turn, o, c : c + 1, :] for o in owners], axis=1)
+                    jnp.concatenate([recv2[turn, o, c : c + 1, :] for o in parts], axis=1)
                     for c in range(2)
                 ]
                 got = mm(rows8(*table), nethot[chunk])
@@ -415,10 +514,18 @@
             total = jnp.concatenate([total, weighed], axis=0)
         arrived = spr_recv[turn]
         both = jnp.concatenate(local, axis=0) + arrived[: terms * tiles] + total
-        summed = jnp.sum(recv2[turn], axis=0)[2:3]
-        wait_all(send_star.at[turn], base + 2)
+        summed = None
+        if not first:
+            wait_all(dot_recv.at[turn], base + 11)
+            summed = jnp.sum(dot_recv[turn], axis=0)
+            wait_all(dot_recv.at[turn], base + 10)
+        for_owner(lambda n: wait_all(send_star.at[turn], base + 2, n * share))
         wait_all(send_cut.at[turn], base + 8)
-        wait_all(recv2.at[turn], base + 6)
+
+        @pl.when(owning)
+        def _():
+            wait_all(recv_star.at[turn], base + 6)
+
         return both, summed
 
     def pick(row, k):
@@ -432,6 +539,7 @@
     def dots_of(pairs):
         return dot_rows([both for a, b in pairs for both in zip(halves_of(a), halves_of(b))])
 
+    load["rs"].wait()
     r = jnp.concatenate(
         [
             rs_ref[c : c + 1, t * LANES : (t + 1) * LANES]
@@ -440,7 +548,7 @@
         ],
         axis=0,
     )
-    both, _ = operate(0, r, lambda: jnp.zeros((1, LANES), F32))
+    both, _ = operate(0, r, None)
     degree = anchor_ref[...] + both[2 * tiles :]
     degree = jnp.concatenate([degree, degree], axis=0)
     w = degree * r - both[: 2 * tiles]
@@ -520,14 +628,23 @@
     per_chunk = count // pin_chunks
     groups = count // GROUP + pin_chunks // GROUP
     wide = GROUP * LANES
+    share = count // ((regions - 2 * (regions // 4)) * halves)
     vmem = pl.BlockSpec(memory_space=pltpu.VMEM)
     shape = jax.ShapeDtypeStruct((4, tiles * LANES), F32)
     joint = pl.pallas_call(
         functools.partial(kernel, regions, halves),
         out_shape=shape,
-        in_specs=[vmem] * 2 + [pl.BlockSpec(memory_space=pl.ANY)] + [vmem] * 6,
+        in_specs=[pl.BlockSpec(memory_space=pl.ANY)] * 9,
         out_specs=vmem,
         scratch_shapes=[
+            pltpu.VMEM(right_side.shape, F32),
+            pltpu.VMEM((tiles, LANES), F32),
+            pltpu.VMEM((near, tiles), jnp.int32),
+            pltpu.VMEM((count, LANES), jnp.int32),
+            pltpu.VMEM((count, LANES), F32),
+            pltpu.VMEM((pin_chunks, LANES), jnp.int32),
+            pltpu.VMEM((pin_chunks, LANES), jnp.int32),
+            pltpu.VMEM((count, LANES), F32),
             pltpu.VMEM((groups, LANES, wide), BF16),
             pltpu.VMEM((groups, tiles, wide), F32),
             pltpu.VMEM((tiles * near, LANES, LANES), F32),
@@ -538,16 +655,20 @@
             pltpu.VMEM((2, tiles, 3 * LANES), F32),
             pltpu.VMEM((3, tiles, LANES), F32),
             pltpu.VMEM((ITERS, count, 2, LANES), F32),
+            pltpu.VMEM((ITERS, count, share, 2, LANES), F32),
             pltpu.VMEM((ITERS, count, 2, LANES), F32),
             pltpu.VMEM((ITERS, count, 2, LANES), F32),
+            pltpu.VMEM((ITERS, share, 2, LANES), F32),
             pltpu.VMEM((ITERS, count, 2, LANES), F32),
-            pltpu.VMEM((ITERS, 4, LANES), F32),
-            pltpu.VMEM((ITERS, count, 4, LANES), F32),
+            pltpu.VMEM((ITERS, 1, LANES), F32),
+            pltpu.VMEM((ITERS, count, 1, LANES), F32),
+            pltpu.VMEM((2, LANES), F32),
             pltpu.VMEM((ITERS, 2 * tiles, LANES), F32),
             pltpu.VMEM((ITERS, 2 * tiles, LANES), F32),
             pltpu.VMEM((ITERS, 3 * tiles, LANES), F32),
             pltpu.VMEM((ITERS, 3 * tiles, LANES), F32),
-            pltpu.SemaphoreType.DMA((10 * ITERS + 1,)),
+            pltpu.SemaphoreType.DMA((12 * ITERS,)),
+            pltpu.SemaphoreType.DMA((9,)),
         ],
         compiler_params=pltpu.CompilerParams(
             collective_id=0, has_side_effects=True, vmem_limit_bytes=56 * 1024 * 1024

time: 47 us -> 43.8 us (0.932)
  Pallas kernels: 44.7 us -> 41.4 us
    pallas_call x1, Pallas kernels: 44.7 us -> 41.4 us  [per_device(): pl.pallas_call(functools.partial(kernel, regions, halves), out_shape=shap...]
where the time goes in v1:
time: 43.8 us; the launch traced here: 43.5 us
  Pallas kernels  41.4 us (95%)
  local copies, waits for them, and re-layouts  1.46 us (3%)
  between operations  0.64 us (1%)
    pallas_call x1, Pallas kernels, per_device(): pl.pallas_call(functools.partial(kernel, regions, halves), out_shape=shap...  41.4 us
    slice x1, local copies, waits for them, and re-layouts, per_device(): return (joint[:2], joint[2:])  1.46 us

profile of v1, /device:TPU:0, one launch (start us, length us, event | category | flops | bytes accessed | tf_op | source)
XLA Modules:
  0.0 43.5 jit_solution(1694814998035237382)
XLA Ops:
  0.6 41.4 %shard_map.104 = f32[4,2048]{1,0:T(4,128)} custom-call(f32[2,2048]{1,0:T(2,128)} %rs_hbm.1, f32[16,128]{1,0:T(8,128)} %bitcast.14, f32[32,128,128]{2,1,0:T(8,128)} %bitcast.8, s32[2,16]{1,0:T(2,128)} %bitcast.15, s32[32,128]{1,0:T(8,128)} %bitcast.9, f32[32,128]{1,0:T(8,128)} %bitcast.10, s32[32,128]{1,0:T(8,128)} %bitcast.11, s32[32,128]{1,0:T(8,128)} %bitcast.12, ...), custom_call_target="tpu_custom_call" | custom-call | tf_op jit(solution)/shard_map/pallas_call | solution.py:634
  42.1 1.5 %fusion = (f32[2,2048]{1,0:T(2,128)}, f32[2,2048]{1,0:T(2,128)}) fusion(f32[4,2048]{1,0:T(4,128)} %shard_map.104), kind=kLoop, calls=%fused_computation | loop fusion | bytes 65536 | tf_op jit(solution)/shard_map/slice | solution.py:687

commit v2 on v1

--- a/solution.py
+++ b/solution.py
@@ -104,25 +104,19 @@
                 half = my_half if flip == 0 else 1 - my_half
                 act(region * halves + half, (region, half))
 
-    def each_owner(act):
-        mine = lax.rem(my_region + owner_regions - first_owner % owner_regions, owner_regions)
-
-        def at(step):
-            place = mine + step
-            return jnp.where(place >= owner_regions, place - owner_regions, place)
-
-        @pl.loop(1, owner_regions, unroll=True if regions <= 16 else 4)
-        def _(step):
-            place = at(step)
-            for flip in range(halves):
-                half = my_half if flip == 0 else 1 - my_half
-                act(place * halves + half, (place + first_owner, half))
-
-        act(mine * halves + 1 - my_half, (mine + first_owner, 1 - my_half))
-
-        @pl.when(jnp.logical_not(owning))
-        def _():
-            act(mine * halves + my_half, (mine + first_owner, my_half))
+    half_owners = owner_regions // 2
+    regions_per_group = owner_regions // pin_groups
+    farthest = half_owners - 1 - lax.rem(my_region, half_owners)
+    farthest = farthest + jnp.where(my_region < regions // 2, half_owners, 0)
+    farthest = farthest // regions_per_group
+
+    def far_first(step):
+        group = 0
+        bit = 1
+        while bit < pin_groups:
+            group = group + lax.rem(farthest // bit + step // bit, 2) * bit
+            bit *= 2
+        return group
 
     def over_groups(groups, body):
         if groups <= 8:
@@ -242,14 +236,37 @@
         )
         return stacked.astype(BF16)
 
+    sub = lax.broadcasted_iota(jnp.int32, (8, wide), 0)
+    in_half = sub < 4
+    in_pair = lax.rem(sub, 4) < 2
+
+    def fold_tiles(rows, mask):
+        rows = rows * mask
+        total = rows[:8]
+        for t in range(8, tiles, 8):
+            total = total + rows[t : t + 8]
+        return total
+
+    def fold_two(a, b):
+        return jnp.where(in_half, a, b) + pltpu.roll(jnp.where(in_half, b, a), 4, 0)
+
     def gathered(group, left):
         got = mm(left, onehot[group])
         got = got[: 2 * tiles] + got[2 * tiles :]
         mask = himask[group]
-        return [
-            jnp.sum(got[c * tiles : (c + 1) * tiles] * mask, axis=0, keepdims=True)
-            for c in range(2)
-        ]
+        both = fold_two(fold_tiles(got[:tiles], mask), fold_tiles(got[tiles:], mask))
+        both = both + pltpu.roll(both, 6, 0)
+        both = both + pltpu.roll(both, 7, 0)
+        return both[0:1], both[4:5]
+
+    def gathered_pieces(group, left):
+        got = mm(left, onehot[group])
+        mask = himask[group]
+        part = [fold_tiles(got[k * tiles : (k + 1) * tiles], mask) for k in range(4)]
+        high = fold_two(part[0], part[1])
+        low = fold_two(part[2], part[3])
+        both = jnp.where(in_pair, high + pltpu.roll(high, 6, 0), low + pltpu.roll(low, 2, 0))
+        return (both + pltpu.roll(both, 7, 0)).astype(BF16)
 
     def scattered(group, rows):
         mask = himask[group]
@@ -307,24 +324,24 @@
         last = turn == ITERS - 1
         terms = 3 if first else 2
         base = turn * 12
-        if first:
-            pl.semaphore_wait(barrier, count - 1)
         vec_send[turn] = vector
-        vec_copy = to_partner(vec_send.at[turn], vec_recv.at[turn], base)
+        if not first:
+            vec_copy = to_partner(vec_send.at[turn], vec_recv.at[turn], base)
         high, low = pieces(vector)
         left = jnp.concatenate([high, low], axis=0)
 
         def star_values(group):
-            rows = gathered(cut_groups + group, left)
+            rows = gathered_pieces(cut_groups + group, left)
             for place in range(GROUP):
                 chunk = group * GROUP + place
-                lanes = slice(place * LANES, (place + 1) * LANES)
-                sums = mm(rows8(rows[0][:, lanes], rows[1][:, lanes]), nethot[chunk], NT)
-                sums = sums[0:2] + sums[2:4]
+                sums = mm(rows[:, place * LANES : (place + 1) * LANES], nethot[chunk], NT)
+                sums = sums + pltpu.roll(sums, 6, 0)
                 for r in range(per_chunk):
-                    send_star[turn, chunk * per_chunk + r] = sums[:, r * LANES : (r + 1) * LANES]
-
-        over_groups(pin_groups, star_values)
+                    lanes = slice(r * LANES, (r + 1) * LANES)
+                    for c in range(2):
+                        send_star[turn, chunk * per_chunk + r, c : c + 1] = sums[
+                            4 * c : 4 * c + 1, lanes
+                        ]
 
         def to_owner(owner, device):
             pltpu.make_async_remote_copy(
@@ -336,13 +353,29 @@
                 device_id_type=MESH,
             ).start()
 
-        each_owner(to_owner)
+        def to_owners_of(group, nearest):
+            for k in range(regions_per_group):
+                place = group * regions_per_group + k
+                act = functools.partial(to_owner, place * halves + my_half)
+                device = (place + first_owner, my_half)
+                to_owner(place * halves + 1 - my_half, (place + first_owner, 1 - my_half))
+                if nearest:
+                    pl.when(place + first_owner != my_region)(functools.partial(act, device))
+                else:
+                    act(device)
+
+        over_groups(pin_groups, star_values)
+        if first:
+            pl.semaphore_wait(barrier, count - 1)
+        for step in range(pin_groups):
+            to_owners_of(far_first(step), step + 1 == pin_groups)
 
         @pl.when(owning)
         def _():
             recv_star[turn, me] = send_star[turn, pl.ds(my_share * share, share)]
 
         if first:
+            vec_copy = to_partner(vec_send.at[turn], vec_recv.at[turn], base)
             load["cut_cell"].wait()
             over_groups(cut_groups, hot_cut)
 
@@ -634,7 +667,7 @@
     joint = pl.pallas_call(
         functools.partial(kernel, regions, halves),
         out_shape=shape,
-        in_specs=[pl.BlockSpec(memory_space=pl.ANY)] * 9,
+        in_specs=[pl.BlockSpec(memory_space=pltpu.HBM)] * 9,
         out_specs=vmem,
         scratch_shapes=[
             pltpu.VMEM(right_side.shape, F32),
@@ -671,9 +704,9 @@
             pltpu.SemaphoreType.DMA((9,)),
         ],
         compiler_params=pltpu.CompilerParams(
-            collective_id=0, has_side_effects=True, vmem_limit_bytes=56 * 1024 * 1024
+            collective_id=0, has_side_effects=True, vmem_limit_bytes=24 * 1024 * 1024
         ),
-    )(
+    )(*[pltpu.with_memory_space_constraint(v, pltpu.HBM) for v in (
         right_side,
         anchor.reshape(tiles, LANES),
         blocks.reshape(tiles * near, LANES, LANES),
@@ -683,7 +716,7 @@
         pin_cell.reshape(pin_chunks, LANES),
         pin_net.reshape(pin_chunks, LANES),
         star_weight.reshape(count, LANES),
-    )
+    )])
     return joint[:2], joint[2:]
 
 

time: 43.8 us -> 40.6 us (0.927)
  Pallas kernels: 41.4 us -> 39.1 us
  local copies, waits for them, and re-layouts: 1.46 us -> 0.62 us
    pallas_call x1, Pallas kernels: 41.4 us -> 39.1 us  [per_device(): pl.pallas_call(functools.partial(kernel, regions, halves), out_shape=shap...]
    slice x1, local copies, waits for them, and re-layouts: 1.46 us -> 0.62 us  [per_device(): return (joint[:2], joint[2:])]
where the time goes in v2:
time: 40.6 us; the launch traced here: 40.3 us
  Pallas kernels  39.1 us (96%)
  between operations  0.64 us (2%)
  local copies, waits for them, and re-layouts  0.62 us (2%)
    pallas_call x1, Pallas kernels, per_device(): pl.pallas_call(functools.partial(kernel, regions, halves), out_shape=shap...  39.1 us

profile of v2, /device:TPU:0, one launch (start us, length us, event | category | flops | bytes accessed | tf_op | source)
XLA Modules:
  0.0 40.3 jit_solution(9650628333437302882)
XLA Ops:
  0.6 39.1 %shard_map.104 = f32[4,2048]{1,0:T(4,128)S(1)} custom-call(f32[2,2048]{1,0:T(2,128)} %rs_hbm.1, f32[16,128]{1,0:T(8,128)} %bitcast.14, f32[32,128,128]{2,1,0:T(8,128)} %bitcast.8, s32[2,16]{1,0:T(2,128)} %bitcast.15, s32[32,128]{1,0:T(8,128)} %bitcast.9, f32[32,128]{1,0:T(8,128)} %bitcast.10, s32[32,128]{1,0:T(8,128)} %bitcast.11, s32[32,128]{1,0:T(8,128)} %bitcast.12, ...), custom_call_target="tpu_custom_call" | custom-call | tf_op jit(solution)/shard_map/pallas_call | solution.py:667
  39.7 0.6 %fusion = (f32[2,2048]{1,0:T(2,128)}, f32[2,2048]{1,0:T(2,128)}) fusion(f32[4,2048]{1,0:T(4,128)S(1)} %shard_map.104), kind=kLoop, calls=%fused_computation | loop fusion | bytes 65536 | tf_op jit(solution)/shard_map/slice | solution.py:720

commit v3 on v2

--- a/solution.py
+++ b/solution.py
@@ -93,16 +93,32 @@
     owning = jnp.logical_and(my_region >= first_owner, my_region < first_owner + owner_regions)
     my_share = (my_region - first_owner) * halves + my_half
 
-    def each_other(act):
-        act(my_region * halves + 1 - my_half, partner)
-
-        @pl.loop(1, regions, unroll=True if regions <= 16 else 4)
+    side = regions // 2
+    my_side = my_region // side
+    my_low = lax.rem(my_region, side)
+    far_count = side * halves
+    near_first = my_side * far_count
+    far_start = (1 - my_side) * far_count
+
+    def each_in(act, first_region, first_step):
+        @pl.loop(first_step, side, unroll=True if regions <= 16 else 4)
         def _(step):
-            region = my_region + step
-            region = jnp.where(region >= regions, region - regions, region)
+            low = my_low + step
+            region = first_region + jnp.where(low >= side, low - side, low)
             for flip in range(halves):
                 half = my_half if flip == 0 else 1 - my_half
                 act(region * halves + half, (region, half))
+
+    def each_far(act):
+        each_in(act, (1 - my_side) * side, 0)
+
+    def each_near(act):
+        each_in(act, my_side * side, 1)
+        act(my_region * halves + 1 - my_half, partner)
+
+    def each_other(act):
+        each_far(act)
+        each_near(act)
 
     half_owners = owner_regions // 2
     regions_per_group = owner_regions // pin_groups
@@ -286,18 +302,18 @@
     def halves_of(x):
         return x[:tiles], x[tiles:]
 
-    def send_all(source_of, target, slot):
+    def send_all(each, source_of, target, sent, arrived):
         def send(other, device):
             pltpu.make_async_remote_copy(
                 src_ref=source_of(other),
                 dst_ref=target.at[me],
-                send_sem=sems.at[slot],
-                recv_sem=sems.at[slot + 1],
+                send_sem=sems.at[sent],
+                recv_sem=sems.at[arrived],
                 device_id=device,
                 device_id_type=MESH,
             ).start()
 
-        each_other(send)
+        each(send)
 
     def wait_all(like, slot, messages=count - 1):
         part = like.at[pl.ds(0, messages)]
@@ -323,7 +339,7 @@
         first = turn == 0
         last = turn == ITERS - 1
         terms = 3 if first else 2
-        base = turn * 12
+        base = turn * 14
         vec_send[turn] = vector
         if not first:
             vec_copy = to_partner(vec_send.at[turn], vec_recv.at[turn], base)
@@ -388,7 +404,8 @@
                 )
 
         over_groups(cut_groups, cut_values)
-        send_all(lambda other: send_cut.at[turn, other], recv_cut.at[turn], base + 8)
+        send_all(each_far, lambda o: send_cut.at[turn, o], recv_cut.at[turn], base + 8, base + 12)
+        send_all(each_near, lambda o: send_cut.at[turn, o], recv_cut.at[turn], base + 8, base + 9)
         recv_cut[turn, me] = send_cut[turn, me]
 
         if first:
@@ -475,23 +492,35 @@
             load["anchor"].wait()
         else:
             dots = dots()
-        wait_all(recv_cut.at[turn], base + 9)
+        wait_all(recv_cut.at[turn], base + 9, far_count - 1)
         if last:
-            across = jnp.sum(
-                send_cut[turn] * recv_cut[turn] * cut_w_ref[...][:, None, :], axis=0
-            )
-            across = across + star_energy[...]
+
+            def across(start):
+                part = pl.ds(start, far_count)
+                terms_of = send_cut[turn, part] * recv_cut[turn, part] * cut_w_ref[part, :][:, None, :]
+                return jnp.sum(terms_of, axis=0)
+
+            near = across(near_first) + star_energy[...]
             energy = []
             for c in range(2):
                 own = vector[c * tiles : (c + 1) * tiles]
                 inner = own * (degree[:tiles] * own - 2.0 * front[c])
-                rows = jnp.sum(inner, axis=0, keepdims=True) - across[c : c + 1]
+                rows = jnp.sum(inner, axis=0, keepdims=True) - near[c : c + 1]
                 energy.append(jnp.sum(rows, axis=1, keepdims=True))
             for c in range(2):
                 dots = jnp.where(lane == 18 + c, energy[c], dots)
         if not first:
-            dot_send[turn] = dots
-            send_all(lambda other: dot_send.at[turn], dot_recv.at[turn], base + 10)
+            dot_send[turn, 0] = dots
+            send_all(each_far, lambda o: dot_send.at[turn, 0], dot_recv.at[turn], base + 10, base + 11)
+        wait_all(recv_cut.at[turn], base + 12, far_count)
+        if last:
+            far = 2.0 * across(far_start)
+            for c in range(2):
+                less = jnp.sum(far[c : c + 1], axis=1, keepdims=True)
+                dots = jnp.where(lane == 18 + c, energy[c] - less, dots)
+        if not first:
+            dot_send[turn, 1] = dots
+            send_all(each_near, lambda o: dot_send.at[turn, 1], dot_recv.at[turn], base + 10, base + 11)
             dot_recv[turn, me] = dots
 
         def cut_group(group, carry):
@@ -693,14 +722,14 @@
             pltpu.VMEM((ITERS, count, 2, LANES), F32),
             pltpu.VMEM((ITERS, share, 2, LANES), F32),
             pltpu.VMEM((ITERS, count, 2, LANES), F32),
-            pltpu.VMEM((ITERS, 1, LANES), F32),
+            pltpu.VMEM((ITERS, 2, 1, LANES), F32),
             pltpu.VMEM((ITERS, count, 1, LANES), F32),
             pltpu.VMEM((2, LANES), F32),
             pltpu.VMEM((ITERS, 2 * tiles, LANES), F32),
             pltpu.VMEM((ITERS, 2 * tiles, LANES), F32),
             pltpu.VMEM((ITERS, 3 * tiles, LANES), F32),
             pltpu.VMEM((ITERS, 3 * tiles, LANES), F32),
-            pltpu.SemaphoreType.DMA((12 * ITERS,)),
+            pltpu.SemaphoreType.DMA((14 * ITERS,)),
             pltpu.SemaphoreType.DMA((9,)),
         ],
         compiler_params=pltpu.CompilerParams(

time: 40.6 us -> 40.3 us (level)
  no operation moved by 1% of the time
where the time goes in v3:
time: 40.3 us; the launch traced here: 40.1 us
  Pallas kernels  38.8 us (96%)
  between operations  0.64 us (2%)
  local copies, waits for them, and re-layouts  0.62 us (2%)
    pallas_call x1, Pallas kernels, per_device(): pl.pallas_call(functools.partial(kernel, regions, halves), out_shape=shap...  38.8 us

profile of v3, /device:TPU:0, one launch (start us, length us, event | category | flops | bytes accessed | tf_op | source)
XLA Modules:
  0.0 40.1 jit_solution(6308747318507743783)
XLA Ops:
  0.6 38.8 %shard_map.104 = f32[4,2048]{1,0:T(4,128)S(1)} custom-call(f32[2,2048]{1,0:T(2,128)} %rs_hbm.1, f32[16,128]{1,0:T(8,128)} %bitcast.14, f32[32,128,128]{2,1,0:T(8,128)} %bitcast.8, s32[2,16]{1,0:T(2,128)} %bitcast.15, s32[32,128]{1,0:T(8,128)} %bitcast.9, f32[32,128]{1,0:T(8,128)} %bitcast.10, s32[32,128]{1,0:T(8,128)} %bitcast.11, s32[32,128]{1,0:T(8,128)} %bitcast.12, ...), custom_call_target="tpu_custom_call" | custom-call | tf_op jit(solution)/shard_map/pallas_call | solution.py:696
  39.4 0.6 %fusion = (f32[2,2048]{1,0:T(2,128)}, f32[2,2048]{1,0:T(2,128)}) fusion(f32[4,2048]{1,0:T(4,128)S(1)} %shard_map.104), kind=kLoop, calls=%fused_computation | loop fusion | bytes 65536 | tf_op jit(solution)/shard_map/slice | solution.py:749

commit v4 on v3

--- a/solution.py
+++ b/solution.py
@@ -54,6 +54,7 @@
     himask,
     block_buf,
     nethot,
+    pinhot,
     quad,
     lhs_b,
     lhs_f,
@@ -346,11 +347,13 @@
         high, low = pieces(vector)
         left = jnp.concatenate([high, low], axis=0)
 
-        def star_values(group):
-            rows = gathered_pieces(cut_groups + group, left)
+        def star_rows(group):
+            return gathered_pieces(cut_groups + group, left)
+
+        def star_sums(group, rows):
             for place in range(GROUP):
                 chunk = group * GROUP + place
-                sums = mm(rows[:, place * LANES : (place + 1) * LANES], nethot[chunk], NT)
+                sums = mm(rows[:, place * LANES : (place + 1) * LANES], *((nethot[chunk], NT) if first else (pinhot[chunk], NN)))
                 sums = sums + pltpu.roll(sums, 6, 0)
                 for r in range(per_chunk):
                     lanes = slice(r * LANES, (r + 1) * LANES)
@@ -380,7 +383,9 @@
                 else:
                     act(device)
 
-        over_groups(pin_groups, star_values)
+        together = [star_rows(group) for group in range(pin_groups)]
+        for group in range(pin_groups):
+            star_sums(group, together[group])
         if first:
             pl.semaphore_wait(barrier, count - 1)
         for step in range(pin_groups):
@@ -409,6 +414,11 @@
         recv_cut[turn, me] = send_cut[turn, me]
 
         if first:
+
+            @pl.loop(0, pin_chunks, unroll=8)
+            def _(chunk):
+                pinhot[chunk] = nethot[chunk].astype(F32).T.astype(BF16)
+
             hold_blocks()
         parts = (*halves_of(high.astype(F32)), *halves_of(low.astype(F32)))
         for r, part in enumerate(parts):
@@ -711,6 +721,7 @@
             pltpu.VMEM((groups, tiles, wide), F32),
             pltpu.VMEM((tiles * near, LANES, LANES), F32),
             pltpu.VMEM((pin_chunks, per_chunk * LANES, LANES), BF16),
+            pltpu.VMEM((pin_chunks, LANES, per_chunk * LANES), BF16),
             pltpu.VMEM((tiles, 2 * LANES, 2 * LANES), BF16),
             pltpu.VMEM((tiles, 8, 2 * LANES), F32),
             pltpu.VMEM((tiles, 8, 2 * LANES), F32),

time: 40.3 us -> 38.3 us (0.950)
  Pallas kernels: 38.8 us -> 36.7 us
    pallas_call x1, Pallas kernels: 38.8 us -> 36.7 us  [per_device(): pl.pallas_call(functools.partial(kernel, regions, halves), out_shape=shap...]
where the time goes in v4:
time: 38.3 us; the launch traced here: 38 us
  Pallas kernels  36.7 us (96%)
  between operations  0.64 us (2%)
  local copies, waits for them, and re-layouts  0.62 us (2%)
    pallas_call x1, Pallas kernels, per_device(): pl.pallas_call(functools.partial(kernel, regions, halves), out_shape=shap...  36.7 us

profile of v4, /device:TPU:0, one launch (start us, length us, event | category | flops | bytes accessed | tf_op | source)
XLA Modules:
  0.0 38.0 jit_solution(14693270130278592773)
XLA Ops:
  0.6 36.7 %shard_map.104 = f32[4,2048]{1,0:T(4,128)S(1)} custom-call(f32[2,2048]{1,0:T(2,128)} %rs_hbm.1, f32[16,128]{1,0:T(8,128)} %bitcast.14, f32[32,128,128]{2,1,0:T(8,128)} %bitcast.8, s32[2,16]{1,0:T(2,128)} %bitcast.15, s32[32,128]{1,0:T(8,128)} %bitcast.9, f32[32,128]{1,0:T(8,128)} %bitcast.10, s32[32,128]{1,0:T(8,128)} %bitcast.11, s32[32,128]{1,0:T(8,128)} %bitcast.12, ...), custom_call_target="tpu_custom_call" | custom-call | tf_op jit(solution)/shard_map/pallas_call | solution.py:706
  37.4 0.6 %fusion = (f32[2,2048]{1,0:T(2,128)}, f32[2,2048]{1,0:T(2,128)}) fusion(f32[4,2048]{1,0:T(4,128)S(1)} %shard_map.104), kind=kLoop, calls=%fused_computation | loop fusion | bytes 65536 | tf_op jit(solution)/shard_map/slice | solution.py:760
